TPU v7x, 32 devices: a whole 2x2x4 slice. The times are simulated.
32 devices in a mesh: rows: 8 (over z, y), band: 4 (over x, core).
Axes of the slice: x: 2, y: 2, z: 4, core: 2. Of those that a mesh axis runs over, the one named last changes fastest.
Arguments:
- coupling: bfloat16 [16384, 2560], P('rows', 'band'), may hold values from -1 to 2
- sketch: bfloat16 [16384, 256], P('rows'), may hold values from -256 to 256
Outputs:
- basis_out: bfloat16 [16384, 256], P(('rows', 'band'))
- factor: float32 [256, 256], replicated
All inputs are finite; a program needn't handle non-finite values.
Results may differ from a plain program's by a relative error of at most 0.015.
Values may be sent and summed in bfloat16 or wider, within the bound.
No kernel may reach another device: no remote copies, remote signals or barrier semaphores. Data moves between devices by JAX's collectives and lax.ppermute only.
A program may use at most 256 MiB of HBM per device.

v0:
```python
import math

import jax
import jax.numpy as jnp
from jax import lax
from jax.sharding import PartitionSpec as P

HB = 1024
TB = 512


def padded_2(block, sides, width):
    for axis, dim in sides:
        count = lax.axis_size(axis)
        forward = [(i, i + 1) for i in range(count - 1)]
        backward = [(target, source) for source, target in forward]
        low = lax.ppermute(
            lax.slice_in_dim(block, block.shape[dim] - width, None, axis=dim), axis, forward
        )
        high = lax.ppermute(lax.slice_in_dim(block, 0, width, axis=dim), axis, backward)
        block = jnp.concatenate([low, block, high], axis=dim)
    return block


def cholesky_upper(gram):
    size = gram.shape[0]
    positions = jnp.arange(size, dtype=jnp.int32)

    def cholesky_step(index, carry):
        work, upper = carry
        work_row = lax.dynamic_index_in_dim(work, index, 0, keepdims=False)
        pivot = jnp.sqrt(lax.dynamic_index_in_dim(work_row, index, 0, keepdims=False))
        row_now = jnp.where(positions >= index, work_row / pivot, jnp.zeros_like(work_row))
        upper = lax.dynamic_update_slice_in_dim(upper, row_now[None, :], index, 0)
        work = work - row_now[:, None] * row_now[None, :]
        return (work, upper)

    start = (gram, jnp.zeros_like(gram))
    return lax.fori_loop(0, size, cholesky_step, start)[1]


def invert_upper(upper):
    size = upper.shape[0]
    positions = jnp.arange(size, dtype=jnp.int32)

    def invert_step(count, solved):
        index = size - 1 - count
        upper_row = lax.dynamic_index_in_dim(upper, index, 0, keepdims=False)
        pivot = lax.dynamic_index_in_dim(upper_row, index, 0, keepdims=False)
        unit_row = jnp.where(
            positions == index, jnp.ones_like(upper_row), jnp.zeros_like(upper_row)
        )
        row_now = (unit_row - jnp.dot(upper_row, solved, precision=lax.Precision.HIGHEST)) / pivot
        return lax.dynamic_update_slice_in_dim(solved, row_now[None, :], index, 0)

    return lax.fori_loop(0, size, invert_step, jnp.zeros_like(upper))


def apply_band(coupling, field):
    rows_dev = field.shape[0]
    width_dev = coupling.shape[1]
    band_index = lax.axis_index("band")
    padded = padded_2(field, (("rows", 0),), HB)
    tile_count = rows_dev // TB
    starts = jnp.arange(tile_count, dtype=jnp.int32) * TB + band_index * width_dev
    windows = jax.vmap(lambda start_row: lax.dynamic_slice_in_dim(padded, start_row, width_dev, 0))(
        starts
    )
    blocks = coupling.reshape(tile_count, TB, width_dev)
    partial_value = jnp.einsum("tiw,twk->tik", blocks, windows, preferred_element_type=jnp.float32)
    return partial_value.reshape(rows_dev, field.shape[1])


def sum_whole(partial_value):
    return lax.psum(partial_value.astype(jnp.bfloat16), "band").astype(jnp.float32)


def per_device(coupling, sketch):
    rows_dev = sketch.shape[0]
    band_count = lax.axis_size("band")
    quarter = rows_dev // band_count
    band_index = lax.axis_index("band")
    rows_total = rows_dev * lax.axis_size("rows")
    first_pass = sum_whole(apply_band(coupling, sketch)).astype(jnp.bfloat16)
    second_full = sum_whole(apply_band(coupling, first_pass))
    second = lax.dynamic_slice_in_dim(second_full, band_index * quarter, quarter, 0)
    local_gram = jnp.dot(
        second.T, second, precision=lax.Precision.HIGHEST, preferred_element_type=jnp.float32
    )
    gram_sum = lax.psum(local_gram, ("rows", "band"))
    upper_factor = cholesky_upper(gram_sum)
    inverse = invert_upper(upper_factor)
    scale_root = math.sqrt(rows_total)
    basis_out = (
        jnp.dot(
            second, inverse, precision=lax.Precision.HIGHEST, preferred_element_type=jnp.float32
        )
        * scale_root
    ).astype(jnp.bfloat16)
    factor = upper_factor / scale_root
    return (basis_out, factor)


def solution(mesh):
    in_specs = (P("rows", "band"), P("rows", None))
    out_specs = (P(("rows", "band"), None), P())
    return jax.shard_map(
        per_device, mesh=mesh, in_specs=in_specs, out_specs=out_specs, check_vma=False
    )
```

profile of v0, /device:TPU:0, one launch (start us, length us, event | category | flops | bytes accessed | tf_op | source)
XLA Modules:
  0.0 1905.1 jit_solution(6150092393344054341)
XLA Ops:
  7.2 2.2 fusion.19
  9.4 5.7 collective-permute-start
  16.5 20.6 %collective-permute-done = bf16[1024,256]{1,0:T(8,128)(2,1)} collective-permute-done((bf16[1024,256]{1,0:T(8,128)(2,1)}, bf16[1024,256]{1,0:T(8,128)(2,1)}, u32[]{:S(2)}, u32[]{:S(2)}) %collective-permute-start) | collective-permute-done | bytes 524320 | tf_op jit(solution)/shard_map/ppermute | solution.py:17
  37.1 3.0 pad_maximum_fusion
  41.2 12.1 while.38
  41.8 2.4 bitcast_dynamic-update-slice_fusion.4
  44.8 2.4 bitcast_dynamic-update-slice_fusion.4
  47.8 2.4 bitcast_dynamic-update-slice_fusion.4
  50.8 2.4 bitcast_dynamic-update-slice_fusion.4
  53.3 3.4 fusion.10
  56.7 2.3 copy.7
  59.0 38.5 %all-reduce.5.cloned.1.call-done = bf16[2048,256]{1,0:T(8,128)(2,1)} async-done(((bf16[2048,256]{1,0:T(8,128)(2,1)}), bf16[2048,256]{1,0:T(8,128)(2,1)}) %all-reduce.5.cloned.1.call-update) | async-done | bytes 1048592 | tf_op jit(solution)/shard_map/psum | solution.py:75
  97.6 2.1 fusion.18
  99.6 4.2 collective-permute-start.2
  105.1 20.1 %collective-permute-done.2 = bf16[1024,256]{1,0:T(8,128)(2,1)} collective-permute-done((bf16[1024,256]{1,0:T(8,128)(2,1)}, bf16[1024,256]{1,0:T(8,128)(2,1)}, u32[]{:S(2)}, u32[]{:S(2)}) %collective-permute-start.2) | collective-permute-done | bytes 524320 | tf_op jit(solution)/shard_map/ppermute | solution.py:17
  125.2 3.0 pad_maximum_fusion.1
  129.3 12.1 while.39
  129.9 2.4 bitcast_dynamic-update-slice_fusion.5
  132.9 2.4 bitcast_dynamic-update-slice_fusion.5
  135.9 2.4 bitcast_dynamic-update-slice_fusion.5
  138.9 2.4 bitcast_dynamic-update-slice_fusion.5
  141.4 3.4 fusion.11
  144.8 2.3 copy.9
  147.1 38.2 %all-reduce.7.cloned.1.call-done = bf16[2048,256]{1,0:T(8,128)(2,1)} async-done(((bf16[2048,256]{1,0:T(8,128)(2,1)}), bf16[2048,256]{1,0:T(8,128)(2,1)}) %all-reduce.7.cloned.1.call-update) | async-done | bytes 1048592 | tf_op jit(solution)/shard_map/psum | solution.py:75
  185.3 2.0 fusion.14
  187.4 131.1 %all-reduce.9.cloned.1.call-done = f32[256,256]{1,0:T(8,128)} async-done(((f32[256,256]{1,0:T(8,128)}), f32[256,256]{1,0:T(8,128)}) %all-reduce.9.cloned.1.call-update) | async-done | bytes 262160 | tf_op jit(solution)/shard_map/psum | solution.py:90
  318.5 1153.1 %while.40 = (s32[]{:T(128)}, f32[256,256]{1,0:T(8,128)}, f32[256,256]{1,0:T(8,128)S(1)}, s32[]{:T(128)}, s32[]{:T(128)}, /*index=5*/s32[]{:T(128)}) while((s32[]{:T(128)}, f32[256,256]{1,0:T(8,128)}, f32[256,256]{1,0:T(8,128)S(1)}, s32[]{:T(128)}, s32[]{:T(128)}, /*index=5*/s32[]{:T(128)}) %tuple.116), condition=%wide.region_4.5_spmd.clone, body=%wide.region_3.4_spmd.clone.sunk | while | flops 132355 | bytes 534141 | solution.py:39
  334.7 1.8 multiply_subtract_fusion.2
  348.2 1.8 multiply_subtract_fusion.2
  366.2 1.8 multiply_subtract_fusion.2
  1472.4 424.2 %while.41 = (s32[]{:T(128)}, f32[256,256]{1,0:T(8,128)S(1)}, f32[256,256]{1,0:T(8,128)S(1)}, s32[]{:T(128)}, s32[]{:T(128)}, /*index=5*/s32[]{:T(128)}, s32[]{:T(128)}) while((s32[]{:T(128)}, f32[256,256]{1,0:T(8,128)S(1)}, f32[256,256]{1,0:T(8,128)S(1)}, s32[]{:T(128)}, s32[]{:T(128)}, /*index=5*/s32[]{:T(128)}, s32[]{:T(128)}) %tuple.119), condition=%wide.region_6.7_spmd.clone, body=%wide.region_5.6_spmd.clone.sunk | while | flops 787463 | bytes 268455 | solution.py:56
  1896.5 2.1 fusion.12
  (2592 shorter events, 1389.4 us)
Async XLA Ops:
  7.2 46.1 %copy-start = (bf16[2048,640]{1,0:T(8,128)(2,1)S(1)}, bf16[2048,640]{1,0:T(8,128)(2,1)}, u32[]{:S(2)}) copy-start(bf16[2048,640]{1,0:T(8,128)(2,1)} %param.6) | copy-start | bytes 7864324
  7.2 90.4 %all-reduce.5.cloned.1.call-start = ((), (), s32[]{:S(2)}) async-start(), calls=%async_computation | async-start | bytes 2097152 | tf_op jit(solution)/shard_map/psum | solution.py:75
  9.4 27.6 %collective-permute-start = (bf16[1024,256]{1,0:T(8,128)(2,1)}, bf16[1024,256]{1,0:T(8,128)(2,1)}, u32[]{:S(2)}, u32[]{:S(2)}) collective-permute-start(bf16[1024,256]{1,0:T(8,128)(2,1)} %get-tuple-element.319), channel_id=1, source_target_pairs={{0,4},{4,8},{8,12},{12,16},{16,20},{20,24},{24,28},{1,5},{5,9},{9,... | collective-permute-start | bytes 1572872 | tf_op jit(solution)/shard_map/ppermute | solution.py:17
  15.2 21.9 %collective-permute-start.1 = (bf16[1024,256]{1,0:T(8,128)(2,1)S(1)}, bf16[1024,256]{1,0:T(8,128)(2,1)}, u32[]{:S(2)}, u32[]{:S(2)}) collective-permute-start(bf16[1024,256]{1,0:T(8,128)(2,1)S(1)} %get-tuple-element.320), channel_id=1, source_target_pairs={{4,0},{8,4},{12,8},{16,12},{20,16},{24,20},{28,24},{5,1},{9,5},{13... | collective-permute-start | bytes 1572872 | tf_op jit(solution)/shard_map/ppermute | solution.py:20
  59.0 126.4 %all-reduce.7.cloned.1.call-start = ((), (), s32[]{:S(2)}) async-start(), calls=%async_computation.1 | async-start | bytes 2097152 | tf_op jit(solution)/shard_map/psum | solution.py:75
  99.6 25.5 %collective-permute-start.2 = (bf16[1024,256]{1,0:T(8,128)(2,1)}, bf16[1024,256]{1,0:T(8,128)(2,1)}, u32[]{:S(2)}, u32[]{:S(2)}) collective-permute-start(bf16[1024,256]{1,0:T(8,128)(2,1)} %get-tuple-element.317), channel_id=1, source_target_pairs={{0,4},{4,8},{8,12},{12,16},{16,20},{20,24},{24,28},{1,5},{5,9},{9,... | collective-permute-start | bytes 1572872 | tf_op jit(solution)/shard_map/ppermute | solution.py:17
  103.8 21.3 %collective-permute-start.3 = (bf16[1024,256]{1,0:T(8,128)(2,1)S(1)}, bf16[1024,256]{1,0:T(8,128)(2,1)}, u32[]{:S(2)}, u32[]{:S(2)}) collective-permute-start(bf16[1024,256]{1,0:T(8,128)(2,1)S(1)} %get-tuple-element.318), channel_id=1, source_target_pairs={{4,0},{8,4},{12,8},{16,12},{20,16},{24,20},{28,24},{5,1},{9,5},{13... | collective-permute-start | bytes 1572872 | tf_op jit(solution)/shard_map/ppermute | solution.py:20
  147.1 171.4 %all-reduce.9.cloned.1.call-start = ((), (), s32[]{:S(2)}) async-start(), calls=%async_computation.2 | async-start | bytes 524288 | tf_op jit(solution)/shard_map/psum | solution.py:90
Sparse Core Ops, SparseCore 0:
  59.1 38.4 all-reduce.4
  147.2 38.1 all-reduce.6
  191.4 127.0 all-reduce.8
where the time goes:
time: 1940 us; the launch traced here: 1910 us
  other arithmetic  822 us (42%)
  local copies, waits for them, and re-layouts  557 us (29%)
  waiting for transfers between devices  249 us (13%)
  loops' own time  193 us (10%)
  matrix products  58.1 us (3%)
    sub x256, other arithmetic, cholesky_step(): work = work - row_now[:, None] * row_now[None, :]  454 us
    dynamic_slice x256, local copies, waits for them, and re-layouts, cholesky_step(): lax.dynamic_index_in_dim(work_row, index, 0, keepdims=False)  324 us
    another operation x1, loops' own time, cholesky_upper(): return lax.fori_loop(0, size, cholesky_step, start)[1]  184 us
    select_n x512, other arithmetic, cholesky_step(): jnp.where(positions >= index, work_row / pivot, jnp.zeros_like(work_row))  183 us
    dynamic_slice x256, local copies, waits for them, and re-layouts, invert_step(): pivot = lax.dynamic_index_in_dim(upper_row, index, 0, keepdims=False)  180 us
    div x256, other arithmetic, invert_step(): (unit_row - jnp.dot(upper_row, solved, precision=lax.Precision.HIGHEST))...  177 us
    psum x1, waiting for transfers between devices, per_device(): gram_sum = lax.psum(local_gram, ('rows', 'band'))  131 us
    psum x2, waiting for transfers between devices, sum_whole(): lax.psum(partial_value.astype(jnp.bfloat16), 'band').astype(jnp.float32)  76.8 us
  transfers between devices with their start and end apart: 7, of which 5 were waited for; matrix products, arithmetic and copies ran while one was open for 0% of the time, Pallas kernels for 0%

commit v1 on v0

v1 whole, which is shorter than its diff:
```python
import functools
import math

import jax
import jax.numpy as jnp
from jax import lax
from jax.experimental import pallas as pl
from jax.experimental.pallas import tpu as pltpu
from jax.sharding import PartitionSpec as P

HB = 1024
TB = 512
HIGHEST = lax.Precision.HIGHEST
F32 = jnp.float32
BF16 = jnp.bfloat16
NB = 64
PIV = 8
VMEM = pl.BlockSpec(memory_space=pltpu.VMEM)
ANY = pl.BlockSpec(memory_space=pl.ANY)


def flip(array, axis, bit):
    count = lax.axis_size(axis)
    return lax.ppermute(array, axis, [(i, i ^ bit) for i in range(count)])


def two_tiles(base, coupling, field_ref, fetched, sems, keep_ref, send_ref):
    width = coupling.shape[1]
    band = lax.axis_index("band")
    half, core = band // 2, band % 2
    copies = []
    for slot in range(2):
        tile = core if slot == 1 else 1 - core
        rows = pl.ds(pl.multiple_of(base + tile * TB, TB), TB)
        copies.append(
            pltpu.make_async_copy(coupling.at[rows, :], fetched.at[slot], sems.at[slot])
        )
    return copies, (band, half, core, width)


def run_tiles(copies, place, field_ref, fetched, keep_ref, send_ref):
    band, half, core, width = place
    for slot, out in ((0, send_ref), (1, keep_ref)):
        tile = core if slot == 1 else 1 - core
        first = pl.multiple_of(tile * TB + band * width - half * HB, 128)
        copies[slot].wait()
        out[...] = jnp.dot(
            fetched[slot], field_ref[pl.ds(first, width), :], preferred_element_type=F32
        ).astype(BF16)


def early_kernel(coupling, field, keep_ref, send_ref, fetched, sems):
    half = lax.axis_index("band") // 2
    copies, place = two_tiles((1 - half) * HB, coupling, field, fetched, sems, keep_ref, send_ref)
    for copy in copies:
        copy.start()
    run_tiles(copies, place, field, fetched, keep_ref, send_ref)


def early_kernel_tiles(coupling, own, own2, far, far2, keep_ref, send_ref, field, fetched, sems):
    band = lax.axis_index("band")
    half, core = band // 2, band % 2
    copies, place = two_tiles((1 - half) * HB, coupling, field, fetched, sems, keep_ref, send_ref)
    for copy in copies:
        copy.start()
    for ref, tile in (
        (own, 2 * half + core),
        (own2, 2 * half + 1 - core),
        (far, 2 * (1 - half) + core),
        (far2, 2 * (1 - half) + 1 - core),
    ):
        field[pl.ds(pl.multiple_of(tile * TB, TB), TB), :] = ref[...]
    run_tiles(copies, place, field, fetched, keep_ref, send_ref)


def late_kernel(coupling, near0, near1, halo, halo2, keep_ref, send_ref, field, fetched, sems):
    band = lax.axis_index("band")
    half, core = band // 2, band % 2
    copies, place = two_tiles(half * HB, coupling, field, fetched, sems, keep_ref, send_ref)
    for copy in copies:
        copy.start()
    near_at, halo_at = (1 - half) * HB, half * HB
    for ref, first in (
        (near0, near_at + core * TB),
        (near1, near_at + (1 - core) * TB),
        (halo, halo_at + core * TB),
        (halo2, halo_at + (1 - core) * TB),
    ):
        field[pl.ds(pl.multiple_of(first, TB), TB), :] = ref[...]
    run_tiles(copies, place, field, fetched, keep_ref, send_ref)


def late_kernel_slab(coupling, slab, halo, halo2, keep_ref, send_ref, field, fetched, sems):
    band = lax.axis_index("band")
    half, core = band // 2, band % 2
    copies, place = two_tiles(half * HB, coupling, field, fetched, sems, keep_ref, send_ref)
    for copy in copies:
        copy.start()
    near_at, halo_at = pl.multiple_of((1 - half) * HB, HB), half * HB
    field[pl.ds(near_at, HB), :] = slab[pl.ds(pl.multiple_of(half * HB, HB), HB), :]
    for ref, first in ((halo, halo_at + core * TB), (halo2, halo_at + (1 - core) * TB)):
        field[pl.ds(pl.multiple_of(first, TB), TB), :] = ref[...]
    run_tiles(copies, place, field, fetched, keep_ref, send_ref)


def product(kernel, coupling, *fields):
    width, columns = coupling.shape[1], fields[0].shape[1]
    scratch = [pltpu.VMEM((2, TB, width), BF16), pltpu.SemaphoreType.DMA((2,))]
    if kernel is not early_kernel:
        scratch = [pltpu.VMEM((2 * HB, columns), BF16)] + scratch
    tile = jax.ShapeDtypeStruct((TB, columns), BF16)
    return pl.pallas_call(
        kernel,
        out_shape=(tile, tile),
        in_specs=[ANY] + [VMEM] * len(fields),
        out_specs=(VMEM, VMEM),
        scratch_shapes=scratch,
        name=kernel.__name__,
        cost_estimate=pl.CostEstimate(
            flops=4 * TB * width * columns, bytes_accessed=4 * TB * width, transcendentals=0
        ),
    )(coupling, *fields)


def gram_kernel(keep, near, far, second_ref, mine_ref, other_ref, packed):
    core = lax.axis_index("band") % 2
    second = keep[...].astype(F32) + near[...].astype(F32) + far[...].astype(F32)
    second_ref[...] = second
    size = second.shape[1]
    mid = size // 2
    over_rows = (((0,), (0,)), ((), ()))
    top = lax.dot_general(
        second[:, :mid], second, over_rows, precision=HIGHEST, preferred_element_type=F32
    )
    low = lax.dot_general(
        second[:, mid:], second[:, mid:], over_rows, precision=HIGHEST, preferred_element_type=F32
    )
    packed[0:mid, :] = top[:, :mid]
    packed[mid:size, :] = top[:, mid:]
    packed[size:, :] = low
    part = 3 * mid // 2
    mine_ref[...] = packed[pl.ds(pl.multiple_of(core * part, 64), part), :]
    other_ref[...] = packed[pl.ds(pl.multiple_of((1 - core) * part, 64), part), :]


def gram(keep, near, far):
    rows, size = keep.shape
    part = jax.ShapeDtypeStruct((3 * size // 4, size // 2), F32)
    return pl.pallas_call(
        gram_kernel,
        out_shape=(jax.ShapeDtypeStruct((rows, size), F32), part, part),
        in_specs=[VMEM] * 3,
        out_specs=(VMEM,) * 3,
        scratch_shapes=[pltpu.VMEM((3 * size // 2, size // 2), F32)],
        name="gram_kernel",
    )(keep, near, far)


def factor_block(block):
    size = block.shape[0]
    groups = size // 8
    rows = [block[8 * i : 8 * i + 8, :] for i in range(groups)]
    shape = rows[0].shape
    sub = lax.broadcasted_iota(jnp.int32, shape, 0)
    for first in range(0, size, PIV):
        own, at = first // 8, first % 8
        pivots = range(PIV)
        row = [jnp.broadcast_to(rows[own][at + p : at + p + 1, :], shape) for p in pivots]
        column = [
            {
                q: jnp.broadcast_to(rows[q][:, first + p : first + p + 1], shape)
                for q in range(own, groups)
            }
            for p in pivots
        ]
        entry = {
            (p, t): jnp.broadcast_to(column[p][own][at + t : at + t + 1, :], shape)
            for p in pivots
            for t in range(p, PIV)
        }
        upper, scale = {}, []
        for p in pivots:
            scale.append(lax.rsqrt(entry[p, p]))
            for t in range(p + 1, PIV):
                upper[p, t] = entry[p, t] * scale[p]
            for t in range(p + 1, PIV):
                for w in range(t, PIV):
                    entry[t, w] = entry[t, w] - upper[p, t] * upper[p, w]

        def solve(values):
            values = list(values)
            for p in pivots:
                values[p] = values[p] * scale[p]
                for t in range(p + 1, PIV):
                    values[t] = values[t] - upper[p, t] * values[p]
            return values

        done = solve(row)
        for q in range(own, groups):
            new = rows[q]
            if PIV < 8 or q > own:
                weight = solve([column[p][q] for p in pivots])
                total = weight[0] * done[0]
                for p in range(1, PIV):
                    total = total + weight[p] * done[p]
                new = new - total
            if q == own:
                new = jnp.where(sub >= at + PIV, new, rows[q])
                for p in pivots:
                    new = jnp.where(sub == at + p, done[p], new)
            rows[q] = new
    return jnp.concatenate(rows, 0)


def factor_kernel(scale_root, mine, other, second, basis_ref, factor_ref, a_ref, b_ref, packed):
    core = lax.axis_index("band") % 2
    part, mid = mine.shape
    size = 2 * mid
    packed[pl.ds(pl.multiple_of(core * part, 64), part), :] = mine[...]
    packed[pl.ds(pl.multiple_of((1 - core) * part, 64), part), :] = other[...]
    a_ref[0:mid, 0:mid] = packed[0:mid, :]
    a_ref[0:mid, mid:size] = packed[mid:size, :]
    a_ref[mid:size, mid:size] = packed[size:, :]
    a_ref[mid:size, 0:mid] = jnp.zeros((mid, mid), F32)
    row_id = lax.broadcasted_iota(jnp.int32, (size, size), 0)
    col_id = lax.broadcasted_iota(jnp.int32, (size, size), 1)
    b_ref[...] = jnp.where(row_id == col_id, 1.0, 0.0).astype(F32)
    factor_ref[...] = jnp.zeros_like(factor_ref)
    lane = lax.broadcasted_iota(jnp.int32, (NB, 128), 1)
    row = lax.broadcasted_iota(jnp.int32, (NB, 128), 0)
    over_rows = (((0,), (0,)), ((), ()))
    for first in range(0, size, NB):
        after = first + NB
        low = (first // 128) * 128
        shift = first - low
        block = a_ref[first:after, low : low + 128]
        if shift:
            block = pltpu.roll(block, 128 - shift, 1)
        block = jnp.where(lane < NB, block, jnp.where(lane - NB == row, 1.0, 0.0))
        block = factor_block(block)
        diagonal = jnp.where((lane < NB) & (lane >= row), block, 0.0)
        if shift:
            diagonal = pltpu.roll(diagonal, shift, 1)
        solve = jnp.where(lane <= row, pltpu.roll(block, 128 - NB, 1), 0.0)[:, :NB]
        high = low + 128
        right = jnp.dot(
            solve, a_ref[first:after, low:size], precision=HIGHEST, preferred_element_type=F32
        )
        column = lax.broadcasted_iota(jnp.int32, right.shape, 1) + low
        right = jnp.where(column >= after, right, 0.0)
        left = jnp.dot(
            solve, b_ref[first:after, 0:high], precision=HIGHEST, preferred_element_type=F32
        )
        if size > high:
            diagonal = jnp.concatenate([diagonal, jnp.zeros((NB, size - high), F32)], 1)
        factor_ref[first:after, low:size] = (right + diagonal) * (1.0 / scale_root)
        b_ref[first:after, 0:high] = left
        if after < size:
            edge = (after // 128) * 128
            ahead = right[:, edge - low :]
            on_a = lax.dot_general(
                ahead, ahead, over_rows, precision=HIGHEST, preferred_element_type=F32
            )
            on_b = lax.dot_general(
                ahead, left, over_rows, precision=HIGHEST, preferred_element_type=F32
            )
            skip = after - edge
            a_ref[after:size, edge:size] -= on_a[skip:, :]
            b_ref[after:size, 0:high] -= on_b[skip:, :]
    basis = lax.dot_general(
        second[...],
        b_ref[...],
        (((1,), (1,)), ((), ())),
        precision=HIGHEST,
        preferred_element_type=F32,
    )
    basis_ref[...] = (basis * scale_root).astype(BF16)


def factor_and_basis(mine, other, second, scale_root):
    rows, size = second.shape
    return pl.pallas_call(
        functools.partial(factor_kernel, scale_root),
        out_shape=(
            jax.ShapeDtypeStruct((rows, size), BF16),
            jax.ShapeDtypeStruct((size, size), F32),
        ),
        in_specs=[VMEM] * 3,
        out_specs=(VMEM, VMEM),
        scratch_shapes=[
            pltpu.VMEM((size, size), F32),
            pltpu.VMEM((size, size), F32),
            pltpu.VMEM((3 * size // 2, size // 2), F32),
        ],
        name="factor_kernel",
    )(mine, other, second)


def halo_step(send):
    slabs, bands = lax.axis_size("rows"), lax.axis_size("band")
    pairs = []
    for r in range(slabs):
        for b in range(bands):
            target = r + 1 if b < bands // 2 else r - 1
            if 0 <= target < slabs:
                pairs.append((r * bands + b, target * bands + b))
    return lax.ppermute(send, ("rows", "band"), pairs)


def inner_step(halo):
    return lax.ppermute(halo, "band", [(1, 0), (2, 3)])


def add16(*parts):
    total = parts[0].astype(F32)
    for part in parts[1:]:
        total = total + part.astype(F32)
    return total.astype(BF16)


def per_device(coupling, sketch):
    slabs = lax.axis_size("rows")
    band = lax.axis_index("band")
    half, core = band // 2, band % 2
    scale_root = math.sqrt(sketch.shape[0] * slabs)

    halo = halo_step(lax.dynamic_slice_in_dim(sketch, (1 - half) * HB + core * TB, TB, 0))
    keep, send = product(early_kernel, coupling, sketch)
    far = flip(add16(keep, flip(send, "band", 1)), "band", 2)
    halo2 = inner_step(halo)
    keep, send = product(late_kernel_slab, coupling, sketch, halo, halo2)
    own = add16(keep, flip(send, "band", 1), far)

    across = flip(own, "band", 2)
    own2 = flip(own, "band", 1)
    halo = halo_step(across)
    across2 = flip(across, "band", 1)
    keep, send = product(early_kernel_tiles, coupling, own, own2, across, across2)
    far = flip(add16(keep, flip(send, "band", 1)), "band", 2)
    halo2 = inner_step(halo)
    keep, send = product(late_kernel, coupling, own, own2, halo, halo2)
    near = flip(send, "band", 1)

    second, mine, other = gram(keep, near, far)
    mine = mine + flip(other, "band", 1)
    mine = mine + flip(mine, "band", 2)
    bit = 1
    while bit < slabs:
        mine = mine + flip(mine, "rows", bit)
        bit *= 2
    other = flip(mine, "band", 1)
    return factor_and_basis(mine, other, second, scale_root)


def solution(mesh):
    in_specs = (P("rows", "band"), P("rows", None))
    out_specs = (P(("rows", "band"), None), P())
    return jax.shard_map(
        per_device, mesh=mesh, in_specs=in_specs, out_specs=out_specs, check_vma=False
    )
```

time: 1940 us -> 99.5 us (0.05); the launches traced: 1910 us -> 98.9 us
  other arithmetic: 822 us -> 4.04 us
  local copies, waits for them, and re-layouts: 557 us -> 5.2 us
  waiting for transfers between devices: 249 us -> 29.6 us
  loops' own time: 193 us -> 0 us
  matrix products: 58.1 us -> 0 us
  Pallas kernels: 0 us -> 31.4 us
    dynamic_slice x512 -> x1, local copies, waits for them, and re-layouts: 504 us -> 0.97 us  [per_device(): lax.dynamic_slice_in_dim(sketch, (1 - half) * HB + core * TB, TB, 0)]
    sub x256 -> x0, other arithmetic: 454 us -> none  [cholesky_step(): work = work - row_now[:, None] * row_now[None, :]]
    psum x3 -> x0, waiting for transfers between devices: 208 us -> none  [the longest x1 131 us: per_device(): gram_sum = lax.psum(local_gram, ('rows', 'band'))]
    another operation x4 -> x0, loops' own time: 193 us -> none  [the longest x1 184 us: cholesky_upper(): return lax.fori_loop(0, size, cholesky_step, start)[1]]
    select_n x513 -> x0, other arithmetic: 183 us -> none  [the longest x512 183 us: cholesky_step(): jnp.where(positions >= index, work_row / pivot, jnp.zeros_like(work_row))]
    div x257 -> x0, other arithmetic: 177 us -> none  [the longest x256 177 us: invert_step(): (unit_row - jnp.dot(upper_row, solved, precision=lax.Precision.HIGHEST))...]
    dot_general x260 -> x0, matrix products: 58.1 us -> none  [the longest x256 47.3 us: invert_step(): jnp.dot(upper_row, solved, precision=lax.Precision.HIGHEST)]
    pallas_call x0 -> x6, Pallas kernels: none -> 31.4 us  [the longest x4 16.7 us: product(): pl.pallas_call(kernel, out_shape=(tile, tile), in_specs=[ANY] + [VMEM] *...]
  transfers between devices with their start and end apart: 7 -> 19, of which waited for: 5 -> 11; matrix products, arithmetic and copies ran while one was open for 0% -> 2% of each run, Pallas kernels for 0% -> 17%
where the time goes in v1:
time: 99.5 us; the launch traced here: 98.9 us
  Pallas kernels  31.4 us (32%)
  waiting for transfers between devices  29.6 us (30%)
  starting transfers between devices  27.8 us (28%)
  local copies, waits for them, and re-layouts  5.2 us (5%)
  other arithmetic  4.04 us (4%)
    ppermute x15, waiting for transfers between devices, flip(): return lax.ppermute(array, axis, [(i, i ^ bit) for i in range(count)])  28 us
    pallas_call x4, Pallas kernels, product(): pl.pallas_call(kernel, out_shape=(tile, tile), in_specs=[ANY] + [VMEM] *...  16.7 us
    ppermute x15, starting transfers between devices, flip(): return lax.ppermute(array, axis, [(i, i ^ bit) for i in range(count)])  15.8 us
    pallas_call x1, Pallas kernels, factor_and_basis(): pl.pallas_call(functools.partial(factor_kernel, scale_root), out_shape=(j...  12.2 us
    ppermute x2, starting transfers between devices, halo_step(): return lax.ppermute(send, ('rows', 'band'), pairs)  9.24 us
    unnamed x24, local copies, waits for them, and re-layouts  4.22 us
    convert_element_type x3, other arithmetic, add16(): return total.astype(BF16)  3.08 us
    ppermute x2, starting transfers between devices, inner_step(): return lax.ppermute(halo, 'band', [(1, 0), (2, 3)])  2.74 us
  transfers between devices with their start and end apart: 19, of which 11 were waited for; matrix products, arithmetic and copies ran while one was open for 2% of the time, Pallas kernels for 17%

profile of v1, /device:TPU:0, one launch (start us, length us, event | category | flops | bytes accessed | tf_op | source)
XLA Modules:
  0.0 98.9 jit_solution(16961397016394324818)
XLA Ops:
  0.7 1.0 constant_dynamic-slice_fusion
  1.6 4.9 %collective-permute-start = (bf16[512,256]{1,0:T(8,128)(2,1)S(1)}, bf16[512,256]{1,0:T(8,128)(2,1)S(1)}, u32[]{:S(2)}, u32[]{:S(2)}) collective-permute-start(bf16[512,256]{1,0:T(8,128)(2,1)S(1)} %constant_dynamic-slice_fusion), channel_id=1, source_target_pairs={{0,4},{1,5},{4,8},{5,9},{6,2},{7,3},{8,12},{9,13},{10,6},{11,7},{1... | collective-permute-start | bytes 786440 | tf_op jit(solution)/shard_map/ppermute | solution.py:307
  6.6 4.1 %early_kernel.1 = (bf16[512,256]{1,0:T(8,128)(2,1)}, bf16[512,256]{1,0:T(8,128)(2,1)}) custom-call(bf16[2048,640]{1,0:T(8,128)(2,1)} %coupling.7, bf16[2048,256]{1,0:T(8,128)(2,1)} %field.1), custom_call_target="tpu_custom_call" | custom-call | flops 335544320 | bytes 1310720 | tf_op jit(solution)/shard_map/early_kernel/pallas_call | solution.py:112
  10.8 1.3 %collective-permute-done.halo = bf16[512,256]{1,0:T(8,128)(2,1)S(1)} collective-permute-done((bf16[512,256]{1,0:T(8,128)(2,1)S(1)}, bf16[512,256]{1,0:T(8,128)(2,1)S(1)}, u32[]{:S(2)}, u32[]{:S(2)}) %collective-permute-start) | collective-permute-done | bytes 262176 | tf_op jit(solution)/shard_map/ppermute | solution.py:307
  12.1 1.3 %collective-permute-start.1 = (bf16[512,256]{1,0:T(8,128)(2,1)S(1)}, bf16[512,256]{1,0:T(8,128)(2,1)S(1)}, u32[]{:S(2)}, u32[]{:S(2)}) collective-permute-start(bf16[512,256]{1,0:T(8,128)(2,1)S(1)} %collective-permute-done.halo), channel_id=1, source_target_pairs={{1,0},{2,3},{5,4},{6,7},{9,8},{10,11},{13,12},{14,15},{17,16},{18,... | collective-permute-start | bytes 786440 | tf_op jit(solution)/shard_map/ppermute | solution.py:311
  13.4 1.0 %add_convert_fusion.2 = bf16[512,256]{1,0:T(8,128)(2,1)S(1)} fusion(bf16[512,256]{1,0:T(8,128)(2,1)S(1)} %collective-permute-done.3, bf16[512,256]{1,0:T(8,128)(2,1)} %get-tuple-element.15), kind=kLoop, calls=%fused_computation.2 | loop fusion | flops 524288 | bytes 786432 | tf_op jit(solution)/shard_map/convert_element_type | solution.py:318
  14.4 2.5 %collective-permute-start.4 = (bf16[512,256]{1,0:T(8,128)(2,1)S(1)}, bf16[512,256]{1,0:T(8,128)(2,1)S(1)}, u32[]{:S(2)}, u32[]{:S(2)}) collective-permute-start(bf16[512,256]{1,0:T(8,128)(2,1)S(1)} %add_convert_fusion.2), channel_id=1, source_target_pairs={{0,2},{1,3},{2,0},{3,1},{4,6},{5,7},{6,4},{7,5},{8,10},{9,11},{10,... | collective-permute-start | bytes 786440 | tf_op jit(solution)/shard_map/ppermute | solution.py:24
  16.9 0.7 copy-done.9
  17.6 4.3 %late_kernel_slab.1 = (bf16[512,256]{1,0:T(8,128)(2,1)}, bf16[512,256]{1,0:T(8,128)(2,1)}) custom-call(bf16[2048,640]{1,0:T(8,128)(2,1)} %coupling.7, bf16[2048,256]{1,0:T(8,128)(2,1)} %field.1, bf16[512,256]{1,0:T(8,128)(2,1)} %copy-done.7, bf16[512,256]{1,0:T(8,128)(2,1)} %copy-done.9), custom_call_target="tpu_custom_call" | custom-call | flops 335544320 | bytes 1310720 | tf_op jit(solution)/shard_map/late_kernel_slab/pallas_call | solution.py:112
  22.0 1.8 %collective-permute-done.4 = bf16[512,256]{1,0:T(8,128)(2,1)S(1)} collective-permute-done((bf16[512,256]{1,0:T(8,128)(2,1)S(1)}, bf16[512,256]{1,0:T(8,128)(2,1)S(1)}, u32[]{:S(2)}, u32[]{:S(2)}) %collective-permute-start.4) | collective-permute-done | bytes 262176 | tf_op jit(solution)/shard_map/ppermute | solution.py:24
  23.8 1.0 %add_convert_fusion.1.near0.own = bf16[512,256]{1,0:T(8,128)(2,1)S(1)} fusion(bf16[512,256]{1,0:T(8,128)(2,1)S(1)} %collective-permute-done.4, bf16[512,256]{1,0:T(8,128)(2,1)S(1)} %collective-permute-done.2, bf16[512,256]{1,0:T(8,128)(2,1)} %get-tuple-element.13), kind=kLoop, calls=%fused_computation.1 | loop fusion | flops 786432 | bytes 1048576 | tf_op jit(solution)/shard_map/convert_element_type | solution.py:318
  25.3 8.0 %collective-permute-done.6.far = bf16[512,256]{1,0:T(8,128)(2,1)S(1)} collective-permute-done((bf16[512,256]{1,0:T(8,128)(2,1)S(1)}, bf16[512,256]{1,0:T(8,128)(2,1)S(1)}, u32[]{:S(2)}, u32[]{:S(2)}) %collective-permute-start.6) | collective-permute-done | bytes 262176 | tf_op jit(solution)/shard_map/ppermute | solution.py:24
  33.2 4.3 %collective-permute-start.7 = (bf16[512,256]{1,0:T(8,128)(2,1)S(1)}, bf16[512,256]{1,0:T(8,128)(2,1)S(1)}, u32[]{:S(2)}, u32[]{:S(2)}) collective-permute-start(bf16[512,256]{1,0:T(8,128)(2,1)S(1)} %collective-permute-done.6.far), channel_id=1, source_target_pairs={{0,4},{1,5},{4,8},{5,9},{6,2},{7,3},{8,12},{9,13},{10,6},{11,7},{1... | collective-permute-start | bytes 786440 | tf_op jit(solution)/shard_map/ppermute | solution.py:307
  38.3 0.7 copy-done.6
  39.0 4.1 %early_kernel_tiles.1 = (bf16[512,256]{1,0:T(8,128)(2,1)}, bf16[512,256]{1,0:T(8,128)(2,1)}) custom-call(bf16[2048,640]{1,0:T(8,128)(2,1)} %coupling.7, bf16[512,256]{1,0:T(8,128)(2,1)} %copy-done, bf16[512,256]{1,0:T(8,128)(2,1)} %copy-done.1, bf16[512,256]{1,0:T(8,128)(2,1)} %copy-done.4, bf16[512,256]{1,0:T(8,128)(2,1)} %copy-done.6), custom_call_target="tpu_custom_call" | custom-call | flops 335544320 | bytes 1310720 | tf_op jit(solution)/shard_map/early_kernel_tiles/pallas_call | solution.py:112
  43.8 1.5 %collective-permute-start.8 = (bf16[512,256]{1,0:T(8,128)(2,1)S(1)}, bf16[512,256]{1,0:T(8,128)(2,1)S(1)}, u32[]{:S(2)}, u32[]{:S(2)}) collective-permute-start(bf16[512,256]{1,0:T(8,128)(2,1)S(1)} %collective-permute-done.7.halo), channel_id=1, source_target_pairs={{1,0},{2,3},{5,4},{6,7},{9,8},{10,11},{13,12},{14,15},{17,16},{18,... | collective-permute-start | bytes 786440 | tf_op jit(solution)/shard_map/ppermute | solution.py:311
  45.2 1.0 %add_convert_fusion = bf16[512,256]{1,0:T(8,128)(2,1)S(1)} fusion(bf16[512,256]{1,0:T(8,128)(2,1)S(1)} %collective-permute-done.11, bf16[512,256]{1,0:T(8,128)(2,1)} %get-tuple-element.19), kind=kLoop, calls=%fused_computation | loop fusion | flops 524288 | bytes 786432 | tf_op jit(solution)/shard_map/convert_element_type | solution.py:318
  46.3 1.7 %collective-permute-start.12 = (bf16[512,256]{1,0:T(8,128)(2,1)S(1)}, bf16[512,256]{1,0:T(8,128)(2,1)S(1)}, u32[]{:S(2)}, u32[]{:S(2)}) collective-permute-start(bf16[512,256]{1,0:T(8,128)(2,1)S(1)} %add_convert_fusion), channel_id=1, source_target_pairs={{0,2},{1,3},{2,0},{3,1},{4,6},{5,7},{6,4},{7,5},{8,10},{9,11},{10,... | collective-permute-start | bytes 786440 | tf_op jit(solution)/shard_map/ppermute | solution.py:24
  48.7 4.1 %late_kernel.1 = (bf16[512,256]{1,0:T(8,128)(2,1)}, bf16[512,256]{1,0:T(8,128)(2,1)}) custom-call(bf16[2048,640]{1,0:T(8,128)(2,1)} %coupling.7, bf16[512,256]{1,0:T(8,128)(2,1)} %copy-done, bf16[512,256]{1,0:T(8,128)(2,1)} %copy-done.1, bf16[512,256]{1,0:T(8,128)(2,1)} %copy-done.3, bf16[512,256]{1,0:T(8,128)(2,1)} %copy-done.5), custom_call_target="tpu_custom_call" | custom-call | flops 335544320 | bytes 1310720 | tf_op jit(solution)/shard_map/late_kernel/pallas_call | solution.py:112
  52.9 2.4 %collective-permute-done.12.far = bf16[512,256]{1,0:T(8,128)(2,1)S(1)} collective-permute-done((bf16[512,256]{1,0:T(8,128)(2,1)S(1)}, bf16[512,256]{1,0:T(8,128)(2,1)S(1)}, u32[]{:S(2)}, u32[]{:S(2)}) %collective-permute-start.12) | collective-permute-done | bytes 262176 | tf_op jit(solution)/shard_map/ppermute | solution.py:24
  56.1 2.5 %gram_kernel.1 = (f32[512,256]{1,0:T(8,128)}, f32[192,128]{1,0:T(8,128)}, f32[192,128]{1,0:T(8,128)}) custom-call(bf16[512,256]{1,0:T(8,128)(2,1)} %get-tuple-element.17.keep, bf16[512,256]{1,0:T(8,128)(2,1)} %copy-done.10, bf16[512,256]{1,0:T(8,128)(2,1)} %copy-done.8), custom_call_target="tpu_custom_call" | custom-call | tf_op jit(solution)/shard_map/gram_kernel/pallas_call | solution.py:149
  58.8 1.4 %collective-permute-done.13 = f32[192,128]{1,0:T(8,128)S(1)} collective-permute-done((f32[192,128]{1,0:T(8,128)}, f32[192,128]{1,0:T(8,128)S(1)}, u32[]{:S(2)}, u32[]{:S(2)}) %collective-permute-start.13) | collective-permute-done | bytes 98336 | tf_op jit(solution)/shard_map/ppermute | solution.py:24
  60.2 0.9 add.45
  61.8 4.2 %collective-permute-done.14 = f32[192,128]{1,0:T(8,128)S(1)} collective-permute-done((f32[192,128]{1,0:T(8,128)S(1)}, f32[192,128]{1,0:T(8,128)S(1)}, u32[]{:S(2)}, u32[]{:S(2)}) %collective-permute-start.14) | collective-permute-done | bytes 98336 | tf_op jit(solution)/shard_map/ppermute | solution.py:24
  66.0 2.5 %collective-permute-start.15 = (f32[192,128]{1,0:T(8,128)S(1)}, f32[192,128]{1,0:T(8,128)S(1)}, u32[]{:S(2)}, u32[]{:S(2)}) collective-permute-start(f32[192,128]{1,0:T(8,128)S(1)} %add.46), channel_id=1, source_target_pairs={{0,4},{4,0},{8,12},{12,8},{16,20},{20,16},{24,28},{28,24},{1,5},{5... | collective-permute-start | bytes 294920 | tf_op jit(solution)/shard_map/ppermute | solution.py:24
  68.5 2.6 %collective-permute-done.15 = f32[192,128]{1,0:T(8,128)S(1)} collective-permute-done((f32[192,128]{1,0:T(8,128)S(1)}, f32[192,128]{1,0:T(8,128)S(1)}, u32[]{:S(2)}, u32[]{:S(2)}) %collective-permute-start.15) | collective-permute-done | bytes 98336 | tf_op jit(solution)/shard_map/ppermute | solution.py:24
  71.2 3.7 %collective-permute-start.16 = (f32[192,128]{1,0:T(8,128)S(1)}, f32[192,128]{1,0:T(8,128)S(1)}, u32[]{:S(2)}, u32[]{:S(2)}) collective-permute-start(f32[192,128]{1,0:T(8,128)S(1)} %add.47), channel_id=1, source_target_pairs={{0,8},{4,12},{8,0},{12,4},{16,24},{20,28},{24,16},{28,20},{1,9},{5... | collective-permute-start | bytes 294920 | tf_op jit(solution)/shard_map/ppermute | solution.py:24
  74.9 2.6 %collective-permute-done.16 = f32[192,128]{1,0:T(8,128)S(1)} collective-permute-done((f32[192,128]{1,0:T(8,128)S(1)}, f32[192,128]{1,0:T(8,128)S(1)}, u32[]{:S(2)}, u32[]{:S(2)}) %collective-permute-start.16) | collective-permute-done | bytes 98336 | tf_op jit(solution)/shard_map/ppermute | solution.py:24
  77.5 3.5 %collective-permute-start.17 = (f32[192,128]{1,0:T(8,128)S(1)}, f32[192,128]{1,0:T(8,128)S(1)}, u32[]{:S(2)}, u32[]{:S(2)}) collective-permute-start(f32[192,128]{1,0:T(8,128)S(1)} %add.48), channel_id=1, source_target_pairs={{0,16},{4,20},{8,24},{12,28},{16,0},{20,4},{24,8},{28,12},{1,17},{... | collective-permute-start | bytes 294920 | tf_op jit(solution)/shard_map/ppermute | solution.py:24
  81.0 3.6 %collective-permute-done.17 = f32[192,128]{1,0:T(8,128)S(1)} collective-permute-done((f32[192,128]{1,0:T(8,128)S(1)}, f32[192,128]{1,0:T(8,128)S(1)}, u32[]{:S(2)}, u32[]{:S(2)}) %collective-permute-start.17) | collective-permute-done | bytes 98336 | tf_op jit(solution)/shard_map/ppermute | solution.py:24
  84.8 1.3 %collective-permute-done.18.other = f32[192,128]{1,0:T(8,128)S(1)} collective-permute-done((f32[192,128]{1,0:T(8,128)S(1)}, f32[192,128]{1,0:T(8,128)S(1)}, u32[]{:S(2)}, u32[]{:S(2)}) %collective-permute-start.18) | collective-permute-done | bytes 98336 | tf_op jit(solution)/shard_map/ppermute | solution.py:24
  86.7 12.2 %factor_kernel.1 = (bf16[512,256]{1,0:T(8,128)(2,1)}, f32[256,256]{1,0:T(8,128)}) custom-call(f32[192,128]{1,0:T(8,128)} %copy-done.2, f32[192,128]{1,0:T(8,128)} %copy-done.11, f32[512,256]{1,0:T(8,128)} %get-tuple-element.23.second), custom_call_target="tpu_custom_call" | custom-call | tf_op jit(solution)/shard_map/factor_kernel/pallas_call | solution.py:282
  (45 shorter events, 5.0 us)
Async XLA Ops:
  1.6 10.5 %collective-permute-start = (bf16[512,256]{1,0:T(8,128)(2,1)S(1)}, bf16[512,256]{1,0:T(8,128)(2,1)S(1)}, u32[]{:S(2)}, u32[]{:S(2)}) collective-permute-start(bf16[512,256]{1,0:T(8,128)(2,1)S(1)} %constant_dynamic-slice_fusion), channel_id=1, source_target_pairs={{0,4},{1,5},{4,8},{5,9},{6,2},{7,3},{8,12},{9,13},{10,6},{11,7},{1... | collective-permute-start | bytes 786440 | tf_op jit(solution)/shard_map/ppermute | solution.py:307
  10.7 2.7 %collective-permute-start.3 = (bf16[512,256]{1,0:T(8,128)(2,1)}, bf16[512,256]{1,0:T(8,128)(2,1)S(1)}, u32[]{:S(2)}, u32[]{:S(2)}) collective-permute-start(bf16[512,256]{1,0:T(8,128)(2,1)} %get-tuple-element.16), channel_id=1, source_target_pairs={{0,1},{1,0},{2,3},{3,2},{4,5},{5,4},{6,7},{7,6},{8,9},{9,8},{10,11... | collective-permute-start | bytes 786440 | tf_op jit(solution)/shard_map/ppermute | solution.py:24
  12.1 4.9 %copy-start.7 = (bf16[512,256]{1,0:T(8,128)(2,1)}, bf16[512,256]{1,0:T(8,128)(2,1)S(1)}, u32[]{:S(2)}) copy-start(bf16[512,256]{1,0:T(8,128)(2,1)S(1)} %collective-permute-done.halo) | copy-start | bytes 786436
  12.1 4.9 %collective-permute-start.1 = (bf16[512,256]{1,0:T(8,128)(2,1)S(1)}, bf16[512,256]{1,0:T(8,128)(2,1)S(1)}, u32[]{:S(2)}, u32[]{:S(2)}) collective-permute-start(bf16[512,256]{1,0:T(8,128)(2,1)S(1)} %collective-permute-done.halo), channel_id=1, source_target_pairs={{1,0},{2,3},{5,4},{6,7},{9,8},{10,11},{13,12},{14,15},{17,16},{18,... | collective-permute-start | bytes 786440 | tf_op jit(solution)/shard_map/ppermute | solution.py:311
  14.4 9.4 %collective-permute-start.4 = (bf16[512,256]{1,0:T(8,128)(2,1)S(1)}, bf16[512,256]{1,0:T(8,128)(2,1)S(1)}, u32[]{:S(2)}, u32[]{:S(2)}) collective-permute-start(bf16[512,256]{1,0:T(8,128)(2,1)S(1)} %add_convert_fusion.2), channel_id=1, source_target_pairs={{0,2},{1,3},{2,0},{3,1},{4,6},{5,7},{6,4},{7,5},{8,10},{9,11},{10,... | collective-permute-start | bytes 786440 | tf_op jit(solution)/shard_map/ppermute | solution.py:24
  16.9 0.7 copy-start.9
  21.9 1.9 %collective-permute-start.2 = (bf16[512,256]{1,0:T(8,128)(2,1)}, bf16[512,256]{1,0:T(8,128)(2,1)S(1)}, u32[]{:S(2)}, u32[]{:S(2)}) collective-permute-start(bf16[512,256]{1,0:T(8,128)(2,1)} %get-tuple-element.14), channel_id=1, source_target_pairs={{0,1},{1,0},{2,3},{3,2},{4,5},{5,4},{6,7},{7,6},{8,9},{9,8},{10,11... | collective-permute-start | bytes 786440 | tf_op jit(solution)/shard_map/ppermute | solution.py:24
  24.9 12.7 %copy-start = (bf16[512,256]{1,0:T(8,128)(2,1)}, bf16[512,256]{1,0:T(8,128)(2,1)S(1)}, u32[]{:S(2)}) copy-start(bf16[512,256]{1,0:T(8,128)(2,1)S(1)} %add_convert_fusion.1.near0.own) | copy-start | bytes 786436
  24.9 8.3 %collective-permute-start.6 = (bf16[512,256]{1,0:T(8,128)(2,1)S(1)}, bf16[512,256]{1,0:T(8,128)(2,1)S(1)}, u32[]{:S(2)}, u32[]{:S(2)}) collective-permute-start(bf16[512,256]{1,0:T(8,128)(2,1)S(1)} %add_convert_fusion.1.near0.own), channel_id=1, source_target_pairs={{0,2},{1,3},{2,0},{3,1},{4,6},{5,7},{6,4},{7,5},{8,10},{9,11},{10,... | collective-permute-start | bytes 786440 | tf_op jit(solution)/shard_map/ppermute | solution.py:24
  25.2 12.3 %collective-permute-start.5 = (bf16[512,256]{1,0:T(8,128)(2,1)S(1)}, bf16[512,256]{1,0:T(8,128)(2,1)S(1)}, u32[]{:S(2)}, u32[]{:S(2)}) collective-permute-start(bf16[512,256]{1,0:T(8,128)(2,1)S(1)} %add_convert_fusion.1.near0.own), channel_id=1, source_target_pairs={{0,1},{1,0},{2,3},{3,2},{4,5},{5,4},{6,7},{7,6},{8,9},{9,8},{10,11... | collective-permute-start | bytes 786440 | tf_op jit(solution)/shard_map/ppermute | solution.py:24
  33.2 4.4 %copy-start.4 = (bf16[512,256]{1,0:T(8,128)(2,1)}, bf16[512,256]{1,0:T(8,128)(2,1)S(1)}, u32[]{:S(2)}) copy-start(bf16[512,256]{1,0:T(8,128)(2,1)S(1)} %collective-permute-done.6.far) | copy-start | bytes 786436
  33.2 4.4 %collective-permute-start.10 = (bf16[512,256]{1,0:T(8,128)(2,1)S(1)}, bf16[512,256]{1,0:T(8,128)(2,1)S(1)}, u32[]{:S(2)}, u32[]{:S(2)}) collective-permute-start(bf16[512,256]{1,0:T(8,128)(2,1)S(1)} %collective-permute-done.6.far), channel_id=1, source_target_pairs={{0,1},{1,0},{2,3},{3,2},{4,5},{5,4},{6,7},{7,6},{8,9},{9,8},{10,11... | collective-permute-start | bytes 786440 | tf_op jit(solution)/shard_map/ppermute | solution.py:24
  33.2 10.5 %collective-permute-start.7 = (bf16[512,256]{1,0:T(8,128)(2,1)S(1)}, bf16[512,256]{1,0:T(8,128)(2,1)S(1)}, u32[]{:S(2)}, u32[]{:S(2)}) collective-permute-start(bf16[512,256]{1,0:T(8,128)(2,1)S(1)} %collective-permute-done.6.far), channel_id=1, source_target_pairs={{0,4},{1,5},{4,8},{5,9},{6,2},{7,3},{8,12},{9,13},{10,6},{11,7},{1... | collective-permute-start | bytes 786440 | tf_op jit(solution)/shard_map/ppermute | solution.py:307
  37.6 0.7 copy-start.1
  38.3 0.7 copy-start.6
  43.1 2.1 %collective-permute-start.11 = (bf16[512,256]{1,0:T(8,128)(2,1)}, bf16[512,256]{1,0:T(8,128)(2,1)S(1)}, u32[]{:S(2)}, u32[]{:S(2)}) collective-permute-start(bf16[512,256]{1,0:T(8,128)(2,1)} %get-tuple-element.20), channel_id=1, source_target_pairs={{0,1},{1,0},{2,3},{3,2},{4,5},{5,4},{6,7},{7,6},{8,9},{9,8},{10,11... | collective-permute-start | bytes 786440 | tf_op jit(solution)/shard_map/ppermute | solution.py:24
  43.8 4.2 %copy-start.3 = (bf16[512,256]{1,0:T(8,128)(2,1)}, bf16[512,256]{1,0:T(8,128)(2,1)S(1)}, u32[]{:S(2)}) copy-start(bf16[512,256]{1,0:T(8,128)(2,1)S(1)} %collective-permute-done.7.halo) | copy-start | bytes 786436
  43.8 4.2 %collective-permute-start.8 = (bf16[512,256]{1,0:T(8,128)(2,1)S(1)}, bf16[512,256]{1,0:T(8,128)(2,1)S(1)}, u32[]{:S(2)}, u32[]{:S(2)}) collective-permute-start(bf16[512,256]{1,0:T(8,128)(2,1)S(1)} %collective-permute-done.7.halo), channel_id=1, source_target_pairs={{1,0},{2,3},{5,4},{6,7},{9,8},{10,11},{13,12},{14,15},{17,16},{18,... | collective-permute-start | bytes 786440 | tf_op jit(solution)/shard_map/ppermute | solution.py:311
  46.3 9.1 %collective-permute-start.12 = (bf16[512,256]{1,0:T(8,128)(2,1)S(1)}, bf16[512,256]{1,0:T(8,128)(2,1)S(1)}, u32[]{:S(2)}, u32[]{:S(2)}) collective-permute-start(bf16[512,256]{1,0:T(8,128)(2,1)S(1)} %add_convert_fusion), channel_id=1, source_target_pairs={{0,2},{1,3},{2,0},{3,1},{4,6},{5,7},{6,4},{7,5},{8,10},{9,11},{10,... | collective-permute-start | bytes 786440 | tf_op jit(solution)/shard_map/ppermute | solution.py:24
  48.0 0.7 copy-start.5
  52.8 2.5 %collective-permute-start.9 = (bf16[512,256]{1,0:T(8,128)(2,1)}, bf16[512,256]{1,0:T(8,128)(2,1)S(1)}, u32[]{:S(2)}, u32[]{:S(2)}) collective-permute-start(bf16[512,256]{1,0:T(8,128)(2,1)} %get-tuple-element.18), channel_id=1, source_target_pairs={{0,1},{1,0},{2,3},{3,2},{4,5},{5,4},{6,7},{7,6},{8,9},{9,8},{10,11... | collective-permute-start | bytes 786440 | tf_op jit(solution)/shard_map/ppermute | solution.py:24
  55.3 0.7 copy-start.8
  55.3 0.8 copy-start.10
  58.6 1.5 %collective-permute-start.13 = (f32[192,128]{1,0:T(8,128)}, f32[192,128]{1,0:T(8,128)S(1)}, u32[]{:S(2)}, u32[]{:S(2)}) collective-permute-start(f32[192,128]{1,0:T(8,128)} %get-tuple-element.22), channel_id=1, source_target_pairs={{0,1},{1,0},{2,3},{3,2},{4,5},{5,4},{6,7},{7,6},{8,9},{9,8},{10,11... | collective-permute-start | bytes 294920 | tf_op jit(solution)/shard_map/ppermute | solution.py:24
  61.1 4.9 %collective-permute-start.14 = (f32[192,128]{1,0:T(8,128)S(1)}, f32[192,128]{1,0:T(8,128)S(1)}, u32[]{:S(2)}, u32[]{:S(2)}) collective-permute-start(f32[192,128]{1,0:T(8,128)S(1)} %add.45), channel_id=1, source_target_pairs={{0,2},{1,3},{2,0},{3,1},{4,6},{5,7},{6,4},{7,5},{8,10},{9,11},{10,... | collective-permute-start | bytes 294920 | tf_op jit(solution)/shard_map/ppermute | solution.py:24
  66.0 5.1 %collective-permute-start.15 = (f32[192,128]{1,0:T(8,128)S(1)}, f32[192,128]{1,0:T(8,128)S(1)}, u32[]{:S(2)}, u32[]{:S(2)}) collective-permute-start(f32[192,128]{1,0:T(8,128)S(1)} %add.46), channel_id=1, source_target_pairs={{0,4},{4,0},{8,12},{12,8},{16,20},{20,16},{24,28},{28,24},{1,5},{5... | collective-permute-start | bytes 294920 | tf_op jit(solution)/shard_map/ppermute | solution.py:24
  71.2 6.3 %collective-permute-start.16 = (f32[192,128]{1,0:T(8,128)S(1)}, f32[192,128]{1,0:T(8,128)S(1)}, u32[]{:S(2)}, u32[]{:S(2)}) collective-permute-start(f32[192,128]{1,0:T(8,128)S(1)} %add.47), channel_id=1, source_target_pairs={{0,8},{4,12},{8,0},{12,4},{16,24},{20,28},{24,16},{28,20},{1,9},{5... | collective-permute-start | bytes 294920 | tf_op jit(solution)/shard_map/ppermute | solution.py:24
  77.5 7.2 %collective-permute-start.17 = (f32[192,128]{1,0:T(8,128)S(1)}, f32[192,128]{1,0:T(8,128)S(1)}, u32[]{:S(2)}, u32[]{:S(2)}) collective-permute-start(f32[192,128]{1,0:T(8,128)S(1)} %add.48), channel_id=1, source_target_pairs={{0,16},{4,20},{8,24},{12,28},{16,0},{20,4},{24,8},{28,12},{1,17},{... | collective-permute-start | bytes 294920 | tf_op jit(solution)/shard_map/ppermute | solution.py:24
  84.7 1.4 %copy-start.2 = (f32[192,128]{1,0:T(8,128)}, f32[192,128]{1,0:T(8,128)S(1)}, u32[]{:S(2)}) copy-start(f32[192,128]{1,0:T(8,128)S(1)} %add.49.mine) | copy-start | bytes 294916
  84.7 1.4 %collective-permute-start.18 = (f32[192,128]{1,0:T(8,128)S(1)}, f32[192,128]{1,0:T(8,128)S(1)}, u32[]{:S(2)}, u32[]{:S(2)}) collective-permute-start(f32[192,128]{1,0:T(8,128)S(1)} %add.49.mine), channel_id=1, source_target_pairs={{0,1},{1,0},{2,3},{3,2},{4,5},{5,4},{6,7},{7,6},{8,9},{9,8},{10,11... | collective-permute-start | bytes 294920 | tf_op jit(solution)/shard_map/ppermute | solution.py:24
  86.1 0.6 copy-start.11
